TPU v7x, 32 devices: a whole 2x2x4 slice. The times are simulated.
32 devices in a mesh: rows: 16 (over z, y, x), cols: 2 (over core).
Axes of the slice: x: 2, y: 2, z: 4, core: 2. Of those that a mesh axis runs over, the one named last changes fastest.
Arguments:
- quantized: bfloat16 [3072, 384, 128], P('rows', 'cols'), may hold values from 0 to 127, as said below
- scales: bfloat16 [3072, 384], P('rows', 'cols'), may hold values from 0 to 1, as said below
- mode_one: float32 [3072, 32], P('rows'), may hold values from 0 to 40
- mode_two: bfloat16 [384, 32], P('cols'), may hold values from 0 to 1, as said below
- mode_three: bfloat16 [4096, 32], replicated, may hold values from 0 to 0.29882812
- core_tensor: float32 [32, 32, 32], P('rows'), may hold values from 0.0002 to 0.004
- slab_index: int32 [1], replicated, may hold values from 0 to 31
Outputs:
- new_one: float32 [3072, 32], P('rows')
- new_core: float32 [32, 32, 32], P('rows')
Inputs may be any that keep to these rules, and one draw needn't show every extreme that they name: `quantized`: nonnegative integer values of an int8 quantization. `scales`: positive. `mode_two`: nonnegative.
All inputs are finite; a program needn't handle non-finite values.
Results may differ from a plain program's by a relative error of at most 0.0017.
Values sent between devices are 32-bit elements; how exact they have to be, the bound alone decides.
A program may use at most 64 MiB of HBM per device.

v0:
```python
import jax
import jax.numpy as jnp
from jax import lax
from jax.sharding import PartitionSpec as P

SLAB = 128


def weight_gram(core_whole, gram_two, gram_three):
    highest = lax.Precision.HIGHEST
    left = jnp.einsum("rab,ac->rcb", core_whole, gram_two, precision=highest)
    left = jnp.einsum("rcb,bd->rcd", left, gram_three, precision=highest)
    flat = core_whole.reshape(core_whole.shape[0], -1)
    return jnp.dot(left.reshape(flat.shape), flat.T, precision=highest)


def hals_sweep(current, target, coupling):
    highest = lax.Precision.HIGHEST

    def column(position, values):
        where = jnp.asarray(position).astype(jnp.int32)
        weights = lax.dynamic_slice_in_dim(coupling, where, 1, 1)[:, 0]
        diagonal = lax.dynamic_index_in_dim(weights, where, 0, keepdims=False)
        wanted = lax.dynamic_slice_in_dim(target, where, 1, 1)[:, 0]
        before = lax.dynamic_slice_in_dim(values, where, 1, 1)[:, 0]
        fitted = jnp.dot(values, weights, precision=highest)
        after = jnp.maximum(before + (wanted - fitted) / diagonal, 0.0)
        return lax.dynamic_update_slice_in_dim(values, after[:, None], where, 1)

    return lax.fori_loop(0, coupling.shape[0], column, current)


def local(quantized, scales, mode_one, mode_two, mode_three, core_tensor, slab_index):
    highest = lax.Precision.HIGHEST
    whole_core = lax.all_gather(core_tensor, "rows", axis=0, tiled=True)
    flat_core = whole_core.reshape(whole_core.shape[0], -1)
    offset = slab_index[0] * SLAB
    chosen = lax.dynamic_slice_in_dim(mode_three, offset, SLAB, 0)
    tensor = quantized * scales[:, :, None]
    folded = jnp.einsum("jr,ijk->irk", mode_two, tensor, preferred_element_type=jnp.float32).astype(
        jnp.bfloat16
    )
    partial_value = jnp.einsum("irk,ks->irs", folded, chosen, preferred_element_type=jnp.float32)
    partial_value = partial_value.reshape(partial_value.shape[0], -1)
    gram_local = jnp.dot(mode_two.T, mode_two, preferred_element_type=jnp.float32)
    gram_three = jnp.dot(chosen.T, chosen, preferred_element_type=jnp.float32)
    local_target = jnp.dot(partial_value, flat_core.T, precision=highest)
    target, gram_two = lax.psum((local_target, gram_local), "cols")
    coupling = weight_gram(whole_core, gram_two, gram_three)
    updated = hals_sweep(mode_one, target, coupling)
    squares = jnp.sum(updated * updated, axis=0)
    counted = mode_one.shape[0] * lax.axis_size("rows")
    totals = lax.psum(squares, "rows")
    spread = jnp.sqrt(totals / counted + 1e-06)
    normed = updated / spread
    local_rank = core_tensor.shape[0]
    owned = lax.dynamic_slice_in_dim(spread, lax.axis_index("rows") * local_rank, local_rank, 0)
    return (normed, core_tensor * owned[:, None, None])


def solution(mesh):
    in_specs = (
        P("rows", "cols", None),
        P("rows", "cols"),
        P("rows", None),
        P("cols", None),
        P(),
        P("rows", None, None),
        P(),
    )
    out_specs = (P("rows", None), P("rows", None, None))
    return jax.shard_map(local, mesh=mesh, in_specs=in_specs, out_specs=out_specs, check_vma=False)
```

profile of v0, /device:TPU:0, one launch (start us, length us, event | category | flops | bytes accessed | tf_op | source)
XLA Modules:
  0.0 148.8 jit_solution(15536030878287488232)
XLA Ops:
  1.4 8.6 %fusion.10 = bf16[192,32,128]{2,1,0:T(8,128)(2,1)S(1)} fusion(bf16[192,192,128]{2,1,0:T(8,128)(2,1)} %param.9, bf16[192,192]{1,0:T(8,128)(2,1)} %param.10, bf16[192,32]{0,1:T(8,128)(2,1)} %param.12), kind=kOutput, calls=%fused_computation.12 | convolution fusion | flops 321650688 | bytes 11096064 | tf_op jit(solution)/shard_map/jr,ijk->irk/dot_general | solution.py:40
  10.0 1.1 fusion.8
  11.1 45.3 %all_gather.3 = f32[32,32,32]{2,1,0:T(8,128)S(1)} all-gather(f32[2,32,32]{2,1,0:T(8,128)S(1)} %copy-done.2), channel_id=1, replica_groups=mesh['rows'=16,'cols'=2] {'rows'}, dimensions={0}, use_global_device_ids=true | all-gather | bytes 139264 | tf_op jit(solution)/shard_map/all_gather | solution.py:35
  56.5 1.1 convolution_bitcast_fusion.1
  57.7 3.5 %all-reduce = (f32[192,32]{0,1:T(8,128)S(1)}, f32[32,32]{1,0:T(8,128)S(1)}) all-reduce(f32[192,32]{0,1:T(8,128)S(1)} %convolution_bitcast_fusion.1, f32[32,32]{1,0:T(8,128)S(1)} %fusion.24), channel_id=1, replica_groups=mesh['rows'=16,'cols'=2] {'cols'}, use_global_device_ids=true, to_apply=%region_1.0 | all-reduce | flops 7168 | bytes 57344 | tf_op jit(solution)/shard_map/psum | solution.py:48
  62.0 0.9 fusion.13
  62.9 0.8 convolution_bitcast_fusion.2
  63.7 46.9 %while.16 = (s32[]{:T(128)}, f32[192,32]{0,1:T(8,128)S(1)}, f32[192,32]{0,1:T(8,128)S(1)}, f32[32,32]{0,1:T(8,128)S(1)}, s32[]{:T(128)}, /*index=5*/s32[]{:T(128)}, s32[]{:T(128)}) while((s32[]{:T(128)}, f32[192,32]{0,1:T(8,128)S(1)}, f32[192,32]{0,1:T(8,128)S(1)}, f32[32,32]{0,1:T(8,128)S(1)}, s32[]{:T(128)}, /*index=5*/s32[]{:T(128)}, ...), condition=%wide.region_3.4_spmd, body=%wide.region_2.3_spmd.sunk | while | flops 74499 | bytes 41849 | solution.py:30
  64.5 0.7 fusion.37
  65.9 0.7 fusion.37
  67.4 0.7 fusion.37
  68.9 0.7 fusion.37
  70.3 0.7 fusion.37
  71.8 0.7 fusion.37
  73.3 0.7 fusion.37
  74.7 0.7 fusion.37
  76.2 0.7 fusion.37
  77.7 0.7 fusion.37
  79.1 0.7 fusion.37
  80.6 0.7 fusion.37
  82.1 0.7 fusion.37
  83.5 0.7 fusion.37
  85.0 0.7 fusion.37
  89.4 0.7 fusion.37
  90.9 0.7 fusion.37
  92.4 0.7 fusion.37
  104.1 0.7 fusion.37
  105.6 0.7 fusion.37
  107.0 0.7 fusion.37
  110.8 36.6 %psum.23 = f32[32]{0:T(128)S(1)} all-reduce(f32[32]{0:T(128)S(1)} %multiply_reduce_fusion), channel_id=1, replica_groups=mesh['rows'=16,'cols'=2] {'rows'}, use_global_device_ids=true, to_apply=%region_5.6 | all-reduce | flops 32 | bytes 256 | tf_op jit(solution)/shard_map/psum | solution.py:53
  147.4 0.7 broadcast_divide_fusion
  148.1 0.7 broadcast_multiply_fusion
  (153 shorter events, 33.2 us)
Async XLA Ops:
  0.6 9.4 %copy-start = (bf16[4096,32]{0,1:T(8,128)(2,1)S(1)}, bf16[4096,32]{0,1:T(8,128)(2,1)}, u32[]{:S(2)}) copy-start(bf16[4096,32]{0,1:T(8,128)(2,1)} %param.13) | copy-start | bytes 786436
  0.6 56.9 %copy-start.3 = (bf16[192,32]{0,1:T(8,128)(2,1)S(1)}, bf16[192,32]{0,1:T(8,128)(2,1)}, u32[]{:S(2)}) copy-start(bf16[192,32]{0,1:T(8,128)(2,1)} %param.12) | copy-start | bytes 36868
  0.7 10.5 %copy-start.2 = (f32[2,32,32]{2,1,0:T(8,128)S(1)}, f32[2,32,32]{2,1,0:T(8,128)}, u32[]{:S(2)}) copy-start(f32[2,32,32]{2,1,0:T(8,128)} %param.14) | copy-start | bytes 24580
  1.4 62.4 %copy-start.1 = (f32[192,32]{0,1:T(8,128)S(1)}, f32[192,32]{0,1:T(8,128)}, u32[]{:S(2)}) copy-start(f32[192,32]{0,1:T(8,128)} %param.11) | copy-start | bytes 73732
where the time goes:
time: 149 us
  blocking collectives  85.5 us (57%)
  other arithmetic  22.3 us (15%)
  local copies, waits for them, and re-layouts  20.7 us (14%)
  matrix products  17.8 us (12%)
    all_gather x1, blocking collectives, local(): whole_core = lax.all_gather(core_tensor, 'rows', axis=0, tiled=True)  45.3 us
    psum x1, blocking collectives, local(): totals = lax.psum(squares, 'rows')  36.6 us
    max x32, other arithmetic, column(): after = jnp.maximum(before + (wanted - fitted) / diagonal, 0.0)  20.8 us
    dynamic_slice x32, local copies, waits for them, and re-layouts, column(): diagonal = lax.dynamic_index_in_dim(weights, where, 0, keepdims=False)  18.9 us
    dot_general x1, matrix products, local(): jnp.einsum('jr,ijk->irk', mode_two, tensor, preferred_element_type=jnp.fl...  8.62 us
    dot_general x32, matrix products, column(): fitted = jnp.dot(values, weights, precision=highest)  4.4 us
    psum x1, blocking collectives, local(): target, gram_two = lax.psum((local_target, gram_local), 'cols')  3.54 us

commit v1 on v0

--- a/solution.py
+++ b/solution.py
@@ -4,6 +4,31 @@
 from jax.sharding import PartitionSpec as P
 
 SLAB = 128
+
+
+def carry_samples(page, array_axis):
+    page = jnp.moveaxis(page, 0, array_axis)
+    taken_in = page.shape
+    return page.reshape(
+        *taken_in[:array_axis],
+        taken_in[array_axis] * taken_in[array_axis + 1],
+        *taken_in[array_axis + 2 :]
+    )
+
+
+def boxes_end(body, mesh_name):
+    axis_len = lax.axis_size(mesh_name)
+    row_out = body[None]
+    for i in range(axis_len.bit_length() - 1):
+        x_now = 1 << i
+        answer = lax.ppermute(
+            row_out, axis_name=mesh_name, perm=[(dev_i, dev_i ^ x_now) for dev_i in range(axis_len)]
+        )
+        aux = jnp.stack([row_out, answer])
+        prior = lax.axis_index(mesh_name)
+        clean = prior >> i & 1
+        row_out = jnp.where(clean == 0, aux, aux[::-1]).reshape(-1, *body.shape)
+    return row_out
 
 
 def weight_gram(core_whole, gram_two, gram_three):
@@ -32,7 +57,8 @@
 
 def local(quantized, scales, mode_one, mode_two, mode_three, core_tensor, slab_index):
     highest = lax.Precision.HIGHEST
-    whole_core = lax.all_gather(core_tensor, "rows", axis=0, tiled=True)
+    out_arr = boxes_end(core_tensor, "rows")
+    whole_core = carry_samples(out_arr, 0)
     flat_core = whole_core.reshape(whole_core.shape[0], -1)
     offset = slab_index[0] * SLAB
     chosen = lax.dynamic_slice_in_dim(mode_three, offset, SLAB, 0)

time: 149 us -> 131 us (0.88)
  blocking collectives: 85.5 us -> 44.5 us
  waiting for transfers between devices: 0 us -> 13.4 us
  starting transfers between devices: 0 us -> 9.52 us
  matrix products: 17.8 us -> 16.3 us
    all_gather x1 -> x0, blocking collectives: 45.3 us -> none  [local(): whole_core = lax.all_gather(core_tensor, 'rows', axis=0, tiled=True)]
    ppermute x0 -> x4, waiting for transfers between devices: none -> 13.4 us  [boxes_end(): lax.ppermute(row_out, axis_name=mesh_name, perm=[(dev_i, dev_i ^ x_now) f...]
    ppermute x0 -> x4, starting transfers between devices: none -> 9.52 us  [boxes_end(): lax.ppermute(row_out, axis_name=mesh_name, perm=[(dev_i, dev_i ^ x_now) f...]
    psum x1, blocking collectives: 36.6 us -> 40.9 us  [local(): totals = lax.psum(squares, 'rows')]
  transfers between devices with their start and end apart: 0 -> 4, of which waited for: 0 -> 3; matrix products, arithmetic and copies ran while one was open for 0% -> 7% of each run, Pallas kernels for 0% -> 0%
where the time goes in v1:
time: 131 us
  blocking collectives  44.5 us (34%)
  other arithmetic  23.3 us (18%)
  local copies, waits for them, and re-layouts  21.2 us (16%)
  matrix products  16.3 us (12%)
  waiting for transfers between devices  13.4 us (10%)
  starting transfers between devices  9.52 us (7%)
  between operations  1.47 us (1%)
    psum x1, blocking collectives, local(): totals = lax.psum(squares, 'rows')  40.9 us
    max x32, other arithmetic, column(): after = jnp.maximum(before + (wanted - fitted) / diagonal, 0.0)  20.8 us
    dynamic_slice x32, local copies, waits for them, and re-layouts, column(): diagonal = lax.dynamic_index_in_dim(weights, where, 0, keepdims=False)  18.9 us
    ppermute x4, waiting for transfers between devices, boxes_end(): lax.ppermute(row_out, axis_name=mesh_name, perm=[(dev_i, dev_i ^ x_now) f...  13.4 us
    ppermute x4, starting transfers between devices, boxes_end(): lax.ppermute(row_out, axis_name=mesh_name, perm=[(dev_i, dev_i ^ x_now) f...  9.52 us
    dot_general x1, matrix products, local(): jnp.einsum('jr,ijk->irk', mode_two, tensor, preferred_element_type=jnp.fl...  8.46 us
    dot_general x32, matrix products, column(): fitted = jnp.dot(values, weights, precision=highest)  4.4 us
    psum x1, blocking collectives, local(): target, gram_two = lax.psum((local_target, gram_local), 'cols')  3.54 us
  transfers between devices with their start and end apart: 4, of which 3 were waited for; matrix products, arithmetic and copies ran while one was open for 7% of the time, Pallas kernels for 0%

profile of v1, /device:TPU:0, one launch (start us, length us, event | category | flops | bytes accessed | tf_op | source)
XLA Modules:
  0.0 130.7 jit_solution(16704111454479774722)
XLA Ops:
  0.7 3.0 %collective-permute-start = (f32[1,2,32,32]{3,2,1,0:T(8,128)}, f32[1,2,32,32]{3,2,1,0:T(8,128)S(1)}, u32[]{:S(2)}, u32[]{:S(2)}) collective-permute-start(f32[1,2,32,32]{3,2,1,0:T(8,128)} %bitcast.69), channel_id=1, source_target_pairs={{0,2},{2,0},{4,6},{6,4},{8,10},{10,8},{12,14},{14,12},{16,18},{18,... | collective-permute-start | bytes 24584 | tf_op jit(solution)/shard_map/ppermute | solution.py:24
  3.7 2.1 %collective-permute-done = f32[1,2,32,32]{3,2,1,0:T(8,128)S(1)} collective-permute-done((f32[1,2,32,32]{3,2,1,0:T(8,128)}, f32[1,2,32,32]{3,2,1,0:T(8,128)S(1)}, u32[]{:S(2)}, u32[]{:S(2)}) %collective-permute-start) | collective-permute-done | bytes 8224 | tf_op jit(solution)/shard_map/ppermute | solution.py:24
  5.8 0.8 pad_maximum_fusion.3
  6.6 2.1 %collective-permute-start.1 = (f32[2,2,32,32]{3,2,1,0:T(8,128)S(1)}, f32[2,2,32,32]{3,2,1,0:T(8,128)S(1)}, u32[]{:S(2)}, u32[]{:S(2)}) collective-permute-start(f32[2,2,32,32]{3,2,1,0:T(8,128)S(1)} %get-tuple-element.148), channel_id=1, source_target_pairs={{0,4},{2,6},{4,0},{6,2},{8,12},{10,14},{12,8},{14,10},{16,20},{18,... | collective-permute-start | bytes 49160 | tf_op jit(solution)/shard_map/ppermute | solution.py:24
  8.7 8.5 %fusion.10 = bf16[192,32,128]{2,1,0:T(8,128)(2,1)S(1)} fusion(bf16[192,192,128]{2,1,0:T(8,128)(2,1)} %param.9, bf16[192,192]{1,0:T(8,128)(2,1)} %param.10, bf16[192,32]{0,1:T(8,128)(2,1)} %param.12), kind=kOutput, calls=%fused_computation.12 | convolution fusion | flops 321650688 | bytes 11096064 | tf_op jit(solution)/shard_map/jr,ijk->irk/dot_general | solution.py:66
  17.9 1.6 %collective-permute-start.2 = (f32[4,2,32,32]{3,2,1,0:T(8,128)S(1)}, f32[4,2,32,32]{3,2,1,0:T(8,128)S(1)}, u32[]{:S(2)}, u32[]{:S(2)}) collective-permute-start(f32[4,2,32,32]{3,2,1,0:T(8,128)S(1)} %bitcast.66), channel_id=1, source_target_pairs={{0,8},{2,10},{4,12},{6,14},{8,0},{10,2},{12,4},{14,6},{16,24},{18,... | collective-permute-start | bytes 98312 | tf_op jit(solution)/shard_map/ppermute | solution.py:24
  19.5 1.1 fusion.8
  20.6 2.3 %collective-permute-done.2 = f32[4,2,32,32]{3,2,1,0:T(8,128)S(1)} collective-permute-done((f32[4,2,32,32]{3,2,1,0:T(8,128)S(1)}, f32[4,2,32,32]{3,2,1,0:T(8,128)S(1)}, u32[]{:S(2)}, u32[]{:S(2)}) %collective-permute-start.2) | collective-permute-done | bytes 32800 | tf_op jit(solution)/shard_map/ppermute | solution.py:24
  23.0 2.8 %collective-permute-start.3 = (f32[8,2,32,32]{3,2,1,0:T(8,128)S(1)}, f32[8,2,32,32]{3,2,1,0:T(8,128)S(1)}, u32[]{:S(2)}, u32[]{:S(2)}) collective-permute-start(f32[8,2,32,32]{3,2,1,0:T(8,128)S(1)} %bitcast.64), channel_id=1, source_target_pairs={{0,16},{2,18},{4,20},{6,22},{8,24},{10,26},{12,28},{14,30},{16,0},... | collective-permute-start | bytes 196616 | tf_op jit(solution)/shard_map/ppermute | solution.py:24
  26.0 9.0 %collective-permute-done.3 = f32[8,2,32,32]{3,2,1,0:T(8,128)S(1)} collective-permute-done((f32[8,2,32,32]{3,2,1,0:T(8,128)S(1)}, f32[8,2,32,32]{3,2,1,0:T(8,128)S(1)}, u32[]{:S(2)}, u32[]{:S(2)}) %collective-permute-start.3) | collective-permute-done | bytes 65568 | tf_op jit(solution)/shard_map/ppermute | solution.py:24
  36.0 3.5 %all-reduce = (f32[192,32]{0,1:T(8,128)S(1)}, f32[32,32]{1,0:T(8,128)S(1)}) all-reduce(f32[192,32]{0,1:T(8,128)S(1)} %fusion.22, f32[32,32]{1,0:T(8,128)S(1)} %fusion.23), channel_id=1, replica_groups=mesh['rows'=16,'cols'=2] {'cols'}, use_global_device_ids=true, to_apply=%region_1.2 | all-reduce | flops 7168 | bytes 57344 | tf_op jit(solution)/shard_map/psum | solution.py:74
  41.3 46.9 %while.16 = (s32[]{:T(128)}, f32[192,32]{0,1:T(8,128)S(1)}, f32[192,32]{0,1:T(8,128)S(1)}, f32[32,32]{0,1:T(8,128)S(1)}, s32[]{:T(128)}, /*index=5*/s32[]{:T(128)}, s32[]{:T(128)}) while((s32[]{:T(128)}, f32[192,32]{0,1:T(8,128)S(1)}, f32[192,32]{0,1:T(8,128)S(1)}, f32[32,32]{0,1:T(8,128)S(1)}, s32[]{:T(128)}, /*index=5*/s32[]{:T(128)}, ...), condition=%wide.region_3.4_spmd, body=%wide.region_2.3_spmd.sunk | while | flops 74499 | bytes 41857 | solution.py:55
  42.0 0.7 fusion.41
  43.5 0.7 fusion.41
  45.0 0.7 fusion.41
  46.4 0.7 fusion.41
  47.9 0.7 fusion.41
  49.4 0.7 fusion.41
  50.8 0.7 fusion.41
  52.3 0.7 fusion.41
  53.8 0.7 fusion.41
  55.2 0.7 fusion.41
  59.6 0.7 fusion.41
  61.1 0.7 fusion.41
  62.6 0.7 fusion.41
  74.3 0.7 fusion.41
  75.8 0.7 fusion.41
  77.2 0.7 fusion.41
  87.5 0.7 fusion.41
  88.3 40.9 %psum.23 = f32[32]{0:T(128)S(1)} all-reduce(f32[32]{0:T(128)S(1)} %multiply_reduce_fusion), channel_id=1, replica_groups=mesh['rows'=16,'cols'=2] {'rows'}, use_global_device_ids=true, to_apply=%region_5.6 | all-reduce | flops 32 | bytes 256 | tf_op jit(solution)/shard_map/psum | solution.py:79
  129.2 0.7 broadcast_divide_fusion
  130.0 0.7 broadcast_multiply_fusion
  (170 shorter events, 37.9 us)
Async XLA Ops:
  0.6 18.9 %copy-start = (bf16[4096,32]{0,1:T(8,128)(2,1)S(1)}, bf16[4096,32]{0,1:T(8,128)(2,1)}, u32[]{:S(2)}) copy-start(bf16[4096,32]{0,1:T(8,128)(2,1)} %param.13) | copy-start | bytes 786436
  0.6 25.1 %copy-start.3 = (bf16[192,32]{0,1:T(8,128)(2,1)S(1)}, bf16[192,32]{0,1:T(8,128)(2,1)}, u32[]{:S(2)}) copy-start(bf16[192,32]{0,1:T(8,128)(2,1)} %param.12) | copy-start | bytes 36868
  0.7 5.1 %collective-permute-start = (f32[1,2,32,32]{3,2,1,0:T(8,128)}, f32[1,2,32,32]{3,2,1,0:T(8,128)S(1)}, u32[]{:S(2)}, u32[]{:S(2)}) collective-permute-start(f32[1,2,32,32]{3,2,1,0:T(8,128)} %bitcast.69), channel_id=1, source_target_pairs={{0,2},{2,0},{4,6},{6,4},{8,10},{10,8},{12,14},{14,12},{16,18},{18,... | collective-permute-start | bytes 24584 | tf_op jit(solution)/shard_map/ppermute | solution.py:24
  6.6 34.7 %copy-start.1 = (f32[192,32]{0,1:T(8,128)S(1)}, f32[192,32]{0,1:T(8,128)}, u32[]{:S(2)}) copy-start(f32[192,32]{0,1:T(8,128)} %param.11) | copy-start | bytes 73732
  6.6 11.3 %collective-permute-start.1 = (f32[2,2,32,32]{3,2,1,0:T(8,128)S(1)}, f32[2,2,32,32]{3,2,1,0:T(8,128)S(1)}, u32[]{:S(2)}, u32[]{:S(2)}) collective-permute-start(f32[2,2,32,32]{3,2,1,0:T(8,128)S(1)} %get-tuple-element.148), channel_id=1, source_target_pairs={{0,4},{2,6},{4,0},{6,2},{8,12},{10,14},{12,8},{14,10},{16,20},{18,... | collective-permute-start | bytes 49160 | tf_op jit(solution)/shard_map/ppermute | solution.py:24
  17.1 112.9 %copy-start.2 = (f32[2,32,32]{2,1,0:T(8,128)S(1)}, f32[2,32,32]{2,1,0:T(8,128)}, u32[]{:S(2)}) copy-start(f32[2,32,32]{2,1,0:T(8,128)} %param.14) | copy-start | bytes 24580
  17.9 5.0 %collective-permute-start.2 = (f32[4,2,32,32]{3,2,1,0:T(8,128)S(1)}, f32[4,2,32,32]{3,2,1,0:T(8,128)S(1)}, u32[]{:S(2)}, u32[]{:S(2)}) collective-permute-start(f32[4,2,32,32]{3,2,1,0:T(8,128)S(1)} %bitcast.66), channel_id=1, source_target_pairs={{0,8},{2,10},{4,12},{6,14},{8,0},{10,2},{12,4},{14,6},{16,24},{18,... | collective-permute-start | bytes 98312 | tf_op jit(solution)/shard_map/ppermute | solution.py:24
  23.0 12.0 %collective-permute-start.3 = (f32[8,2,32,32]{3,2,1,0:T(8,128)S(1)}, f32[8,2,32,32]{3,2,1,0:T(8,128)S(1)}, u32[]{:S(2)}, u32[]{:S(2)}) collective-permute-start(f32[8,2,32,32]{3,2,1,0:T(8,128)S(1)} %bitcast.64), channel_id=1, source_target_pairs={{0,16},{2,18},{4,20},{6,22},{8,24},{10,26},{12,28},{14,30},{16,0},... | collective-permute-start | bytes 196616 | tf_op jit(solution)/shard_map/ppermute | solution.py:24
